TPU v7x, 256 devices: a whole 4x4x8 slice. The times are simulated.
256 devices in a mesh: dp: 64 (over x, z, core), rep: 4 (over y).
Axes of the slice: x: 4, y: 4, z: 8, core: 2. Of those that a mesh axis runs over, the one named last changes fastest.
Arguments:
- frames_in: bfloat16 [4, 57344, 1536], P('rep', 'dp')
- lengths: int32 [4, 64, 4], P('rep', 'dp'), may hold values from 1 to 893, as said below
- norm_gain: float32 [1536], replicated, may hold values from 0.5 to 1.5
- norm_bias: float32 [1536], replicated, may hold values from -2 to 2
- w_in: bfloat16 [1536, 3072], P(('dp', 'rep')), may hold values from -0.15625 to 0.15625
- kernel: float32 [31, 1536], replicated, may hold values from -1 to 1
- batch_gain: float32 [1536], replicated, may hold values from 0.5 to 1.5
- batch_bias: float32 [1536], replicated, may hold values from -3 to 3
- w_out: bfloat16 [1536, 1536], P(('dp', 'rep')), may hold values from -0.15625 to 0.15625
Outputs:
- frames_out: bfloat16 [4, 57344, 1536], P('rep', 'dp')
Inputs may be any that keep to these rules, and one draw needn't show every extreme that they name: `lengths`: for each rep index, the devices 2k and 2k + 1 of dp hold 1024 frames together, so each rep index holds 512 frames for each of its dp devices; a device holds at most 896 frames, and some device of every rep index holds exactly 896.
All inputs are finite; a program needn't handle non-finite values.
Results may differ from a plain program's by a relative error of at most 0.0038.
Values may be sent and summed in bfloat16 or wider, within the bound.
A program may use at most 128 MiB of HBM per device.

v0:
```python
import jax
import jax.numpy as jnp
from jax import lax
from jax.sharding import PartitionSpec as P

FR_DEV = 512
EPSILON = 1e-05


def layer_norm(frames, norm_gain, norm_bias):
    values = frames.astype(jnp.float32)
    average = jnp.mean(values, axis=-1, keepdims=True)
    centred = values - average
    spread = jnp.mean(centred * centred, axis=-1, keepdims=True)
    return centred * lax.rsqrt(spread + EPSILON) * norm_gain + norm_bias


def depthwise(gated, labels, kernel):
    half_kernel = kernel.shape[0] // 2
    length_rows = gated.shape[0]
    padded = jnp.pad(gated, ((half_kernel, half_kernel), (0, 0)))
    padded_labels = jnp.pad(labels, (half_kernel, half_kernel), constant_values=-1)
    summed = jnp.zeros(gated.shape, jnp.float32)
    for offset in range(kernel.shape[0]):
        shared = padded_labels[offset : offset + length_rows] == labels
        contribution = jnp.where(
            shared[:, None], padded[offset : offset + length_rows].astype(jnp.float32), 0.0
        )
        summed = summed + contribution * kernel[offset]
    return summed


def project_in(normed, weight_rows):
    return jnp.dot(normed, weight_rows, preferred_element_type=jnp.float32)


def project_out(active, weight_rows):
    return jnp.dot(active, weight_rows, preferred_element_type=jnp.float32)


def on_device(
    frames_in, lengths, norm_gain, norm_bias, w_in, kernel, batch_gain, batch_bias, w_out
):
    local_frames = frames_in[0]
    local_lengths = lengths[0, 0]
    capacity = local_frames.shape[0]
    features = local_frames.shape[1]
    total_count = lax.axis_size("dp") * lax.axis_size("rep") * FR_DEV
    grouped = (w_in, w_out)
    grouped = (
        lax.all_gather(w_in, ("dp", "rep"), axis=0, tiled=True),
        lax.all_gather(w_out, ("dp", "rep"), axis=0, tiled=True),
    )
    rows_here = jnp.arange(capacity, dtype=jnp.int32)
    local_load = jnp.sum(local_lengths)
    bounds = jnp.cumsum(local_lengths)
    labels = jnp.sum((rows_here[:, None] >= bounds[None, :]).astype(jnp.int32), axis=1)
    row_weight = (rows_here < local_load).astype(jnp.float32)[:, None]
    normed = layer_norm(local_frames, norm_gain, norm_bias).astype(jnp.bfloat16)
    projected = project_in(normed, grouped[0])
    gated = (projected[:, :features] * jax.nn.sigmoid(projected[:, features:])).astype(jnp.bfloat16)
    convolved = depthwise(gated, labels, kernel)
    average = lax.psum(jnp.sum(convolved * row_weight, axis=0), ("dp", "rep")) / total_count
    centred = convolved - average
    spread = lax.psum(jnp.sum(centred * centred * row_weight, axis=0), ("dp", "rep")) / total_count
    scaled = centred * lax.rsqrt(spread + EPSILON) * batch_gain + batch_bias
    active = jax.nn.silu(scaled).astype(jnp.bfloat16)
    branch = project_out(active, grouped[1])
    mixed = (local_frames.astype(jnp.float32) + branch).astype(jnp.bfloat16)
    result = jnp.where(rows_here[:, None] < local_load, mixed, jnp.zeros_like(mixed))
    return result[None]


def solution(mesh):
    placed = (
        P("rep", "dp", None),
        P("rep", "dp", None),
        P(),
        P(),
        P(("dp", "rep"), None),
        P(),
        P(),
        P(),
        P(("dp", "rep"), None),
    )
    return jax.shard_map(
        on_device, mesh=mesh, in_specs=placed, out_specs=P("rep", "dp", None), check_vma=False
    )
```

profile of v0, /device:TPU:1, one launch (start us, length us, event | category | flops | bytes accessed | tf_op | source)
XLA Modules:
  0.0 487.7 jit_solution(4124133330554323458)
XLA Ops:
  6.5 0.0 all-gather.7.cloned.1.call-start
  6.5 0.7 all-gather.7.cloned.1.call-update
  7.3 0.0 all-gather.5.cloned.1.call-start
  7.3 0.7 all-gather.5.cloned.1.call-update
  8.0 1.3 reduce_sum.54
  9.3 0.8 reduce-window.8
  10.1 0.6 iota_compare_fusion.1
  10.8 0.7 fusion.26
  11.4 0.1 convert_reduce_fusion.1
  11.5 1.5 slice_reduce_fusion.29
  13.0 1.8 slice_reduce_fusion.30
  14.9 0.1 slice_compare_fusion.26
  14.9 2.2 convert_reduce_fusion
  17.2 2.6 fusion.4
  19.8 0.1 slice_compare_fusion.29
  19.9 0.1 slice_compare_fusion.28
  20.0 0.1 slice_compare_fusion.27
  20.1 111.2 %all-gather.7.cloned.1.call-done = bf16[256,6,1536]{2,1,0:T(8,128)(2,1)} async-done(((bf16[1,6,1536]{2,1,0:T(8,128)(2,1)}), bf16[256,6,1536]{2,1,0:T(8,128)(2,1)}) %all-gather.7.cloned.1.call-update) | async-done | bytes 4718608 | tf_op jit(solution)/shard_map/all_gather | solution.py:52
  131.3 8.5 %reshape.87 = bf16[1536,1536]{1,0:T(8,128)(2,1)} reshape(bf16[256,6,1536]{2,1,0:T(8,128)(2,1)} %all-gather.7.cloned.1.call-done) | data formatting | bytes 9437184
  139.8 0.0 copy-start
  139.8 0.0 copy-start.2
  139.8 0.0 copy-start.3
  139.8 113.5 %all-gather.5.cloned.1.call-done = bf16[256,6,3072]{2,1,0:T(8,128)(2,1)} async-done(((bf16[1,6,3072]{2,1,0:T(8,128)(2,1)}), bf16[256,6,3072]{2,1,0:T(8,128)(2,1)}) %all-gather.5.cloned.1.call-update) | async-done | bytes 9437200 | tf_op jit(solution)/shard_map/all_gather | solution.py:51
  253.3 14.2 %reshape.85 = bf16[1536,3072]{1,0:T(8,128)(2,1)} reshape(bf16[256,6,3072]{2,1,0:T(8,128)(2,1)} %all-gather.5.cloned.1.call-done) | data formatting | bytes 18874368
  267.5 0.0 copy-done
  267.5 0.0 copy-done.2
  267.5 0.0 copy-done.3
  267.5 11.3 %fusion.16 = f32[896,3072]{1,0:T(8,128)S(1)} fusion(bf16[1536,3072]{1,0:T(8,128)(2,1)} %reshape.85, bf16[1,896,1536]{2,1,0:T(8,128)(2,1)S(1)} %copy-done, f32[1536]{0:T(1024)S(1)} %copy-done.2, f32[1536]{0:T(1024)S(1)} %copy-done.3, f32[896]{0:T(1024)S(1)} %add_rsqrt_fusion.1, f32[896]{0:T(1024)S(1)} %broadcast_multiply_fusion.1), kind=kOutput, calls=%fused_computation.23 | convolution fusion | flops 8463974400 | bytes 23219200 | tf_op jit(solution)/shard_map/dot_general | solution.py:34
  278.8 1.5 fusion.13
  280.4 0.0 copy-start.4
  280.4 0.0 copy-start.5
  280.4 38.3 %multiply_reduce_fusion.1 = (f32[1536]{0:T(1024)S(1)}, f32[896,1536]{1,0:T(8,128)}) fusion(f32[896]{0:T(1024)S(1)} %fusion.26, f32[1536]{0:T(1024)S(1)} %get-tuple-element.34, pred[896]{0:T(1024)(128)(4,1)S(1)} %get-tuple-element.67, f32[1536]{0:T(1024)S(1)} %get-tuple-element.35, pred[896]{0:T(1024)(128)(4,1)S(1)} %get-tuple-element.39, ...), kind=kLoop, calls=%fused_computation.18 | loop fusion | flops 170654208 | bytes 8484608 | tf_op jit(solution)/shard_map/reduce_sum | solution.py:63
  318.7 0.0 copy-start.1
  318.7 74.8 %psum.14 = f32[1536]{0:T(1024)S(1)} all-reduce(f32[1536]{0:T(1024)S(1)} %get-tuple-element.36), channel_id=1, replica_groups=mesh['dp'=64,'rep'=4] {'dp','rep'}, use_global_device_ids=true, to_apply=%region_6.7 | all-reduce | flops 1536 | bytes 12288 | tf_op jit(solution)/shard_map/psum | solution.py:63
  393.5 3.3 multiply_reduce_fusion
  396.8 73.6 %psum.15 = f32[1536]{0:T(1024)S(1)} all-reduce(f32[1536]{0:T(1024)S(1)} %multiply_reduce_fusion), channel_id=1, replica_groups=mesh['dp'=64,'rep'=4] {'dp','rep'}, use_global_device_ids=true, to_apply=%region_8.9 | all-reduce | flops 1536 | bytes 12288 | tf_op jit(solution)/shard_map/psum | solution.py:65
  470.4 0.0 copy-done.4
  470.4 0.0 copy-done.5
  470.4 0.0 copy-done.1
  470.4 10.4 %fusion.15 = bf16[1,896,1536]{2,1,0:T(8,128)(2,1)} fusion(bf16[1536,1536]{1,0:T(8,128)(2,1)} %reshape.87, bf16[1,896,1536]{2,1,0:T(8,128)(2,1)S(1)} %copy-done.1, f32[896,1536]{1,0:T(8,128)} %get-tuple-element.37, f32[1536]{0:T(1024)S(1)} %copy-done.4, f32[1536]{0:T(1024)S(1)} %copy-done.5, f32[1536]{0:T(1024)S(1)} %add_rsqrt_fusion, ...), kind=kOutput, calls=%fused_computation.22 | convolution fusion | flops 4245749760 | bytes 15754112 | tf_op jit(solution)/shard_map/dot_general | solution.py:38
  (4 shorter events, 0.0 us)
Async XLA Ops:
  6.5 124.8 %all-gather.7.cloned.1.call-start = ((), (), s32[]{:S(2)}) async-start(), calls=%async_computation.1 | async-start | bytes 6316032 | tf_op jit(solution)/shard_map/all_gather | solution.py:52
  7.3 246.1 %all-gather.5.cloned.1.call-start = ((), (), s32[]{:S(2)}) async-start(), calls=%async_computation | async-start | bytes 12632064 | tf_op jit(solution)/shard_map/all_gather | solution.py:51
  139.8 127.7 %copy-start = (bf16[1,896,1536]{2,1,0:T(8,128)(2,1)S(1)}, bf16[1,896,1536]{2,1,0:T(8,128)(2,1)}, u32[]{:S(2)}) copy-start(bf16[1,896,1536]{2,1,0:T(8,128)(2,1)} %param.9) | copy-start | bytes 8257540
  139.8 127.7 %copy-start.2 = (f32[1536]{0:T(1024)S(1)}, f32[1536]{0:T(1024)}, u32[]{:S(2)}) copy-start(f32[1536]{0:T(1024)} %param.12) | copy-start | bytes 18436
  139.8 127.7 %copy-start.3 = (f32[1536]{0:T(1024)S(1)}, f32[1536]{0:T(1024)}, u32[]{:S(2)}) copy-start(f32[1536]{0:T(1024)} %param.11) | copy-start | bytes 18436
  280.4 190.1 %copy-start.4 = (f32[1536]{0:T(1024)S(1)}, f32[1536]{0:T(1024)}, u32[]{:S(2)}) copy-start(f32[1536]{0:T(1024)} %param.16) | copy-start | bytes 18436
  280.4 190.1 %copy-start.5 = (f32[1536]{0:T(1024)S(1)}, f32[1536]{0:T(1024)}, u32[]{:S(2)}) copy-start(f32[1536]{0:T(1024)} %param.15) | copy-start | bytes 18436
  318.7 151.7 %copy-start.1 = (bf16[1,896,1536]{2,1,0:T(8,128)(2,1)S(1)}, bf16[1,896,1536]{2,1,0:T(8,128)(2,1)}, u32[]{:S(2)}) copy-start(bf16[1,896,1536]{2,1,0:T(8,128)(2,1)} %param.9) | copy-start | bytes 8257540
Sparse Core Ops, SparseCore 0:
  11.2 120.0 all-gather.6
  135.1 118.1 all-gather.4
where the time goes:
time: 489 us; the launch traced here: 488 us
  waiting for transfers between devices  226 us (46%)
  blocking collectives  148 us (30%)
  other arithmetic  51.8 us (11%)
  local copies, waits for them, and re-layouts  26 us (5%)
  matrix products  21.8 us (4%)
  between operations  13.5 us (3%)
    all_gather x1, waiting for transfers between devices, on_device(): lax.all_gather(w_in, ('dp', 'rep'), axis=0, tiled=True)  114 us
    all_gather x1, waiting for transfers between devices, on_device(): lax.all_gather(w_out, ('dp', 'rep'), axis=0, tiled=True)  111 us
    psum x1, blocking collectives, on_device(): lax.psum(jnp.sum(convolved * row_weight, axis=0), ('dp', 'rep'))  74.8 us
    psum x1, blocking collectives, on_device(): lax.psum(jnp.sum(centred * centred * row_weight, axis=0), ('dp', 'rep'))  73.6 us
    reduce_sum x1, other arithmetic, on_device(): jnp.sum(convolved * row_weight, axis=0)  38.3 us
    unnamed x14, local copies, waits for them, and re-layouts  22.6 us
    dot_general x1, matrix products, project_in(): return jnp.dot(normed, weight_rows, preferred_element_type=jnp.float32)  11.3 us
    dot_general x1, matrix products, project_out(): return jnp.dot(active, weight_rows, preferred_element_type=jnp.float32)  10.4 us
  transfers between devices with their start and end apart: 2, of which 2 were waited for; matrix products, arithmetic and copies ran while one was open for 4% of the time, Pallas kernels for 0%

commit v1 on v0

--- a/solution.py
+++ b/solution.py
@@ -5,6 +5,12 @@
 
 FR_DEV = 512
 EPSILON = 1e-05
+
+
+def _reach_zones(vec, net_axis):
+    opened = jax.lax.all_to_all(jnp.stack(jax.lax.axis_size(net_axis) * [vec], 0), net_axis, 0, 0)
+    long_array = jnp.concatenate(opened, 0)
+    return long_array
 
 
 def layer_norm(frames, norm_gain, norm_bias):
@@ -48,7 +54,7 @@
     total_count = lax.axis_size("dp") * lax.axis_size("rep") * FR_DEV
     grouped = (w_in, w_out)
     grouped = (
-        lax.all_gather(w_in, ("dp", "rep"), axis=0, tiled=True),
+        _reach_zones(w_in, ("dp", "rep")),
         lax.all_gather(w_out, ("dp", "rep"), axis=0, tiled=True),
     )
     rows_here = jnp.arange(capacity, dtype=jnp.int32)

time: 489 us -> 555 us (1.13)
  waiting for transfers between devices: 226 us -> 278 us
  starting transfers between devices: 0.04 us -> 16.6 us
    all_to_all x0 -> x1, waiting for transfers between devices: none -> 130 us  [_reach_zones(): jax.lax.all_to_all(jnp.stack(jax.lax.axis_size(net_axis) * [vec], 0), net...]
    all_gather x1 -> x0, waiting for transfers between devices: 114 us -> none  [on_device(): lax.all_gather(w_in, ('dp', 'rep'), axis=0, tiled=True)]
    all_gather x1, waiting for transfers between devices: 111 us -> 147 us  [on_device(): lax.all_gather(w_out, ('dp', 'rep'), axis=0, tiled=True)]
    all_to_all x0 -> x1, starting transfers between devices: none -> 16.5 us  [_reach_zones(): jax.lax.all_to_all(jnp.stack(jax.lax.axis_size(net_axis) * [vec], 0), net...]
    unnamed x14 -> x17, local copies, waits for them, and re-layouts: 22.6 us -> 8.43 us
    reshape x0 -> x1, local copies, waits for them, and re-layouts: none -> 14.2 us  [_reach_zones(): long_array = jnp.concatenate(opened, 0)]
    another operation x0 -> x1, local copies, waits for them, and re-layouts: none -> 6.86 us  [_reach_zones(): jnp.stack(jax.lax.axis_size(net_axis) * [vec], 0)]
  transfers between devices with their start and end apart: 2 -> 2, of which waited for: 2 -> 2; matrix products, arithmetic and copies ran while one was open for 4% -> 2% of each run, Pallas kernels for 0% -> 0%
where the time goes in v1:
time: 555 us; the launch traced here: 554 us
  waiting for transfers between devices  278 us (50%)
  blocking collectives  147 us (26%)
  other arithmetic  46.9 us (8%)
  local copies, waits for them, and re-layouts  30 us (5%)
  matrix products  21.8 us (4%)
  starting transfers between devices  16.6 us (3%)
  between operations  13.5 us (2%)
    all_gather x1, waiting for transfers between devices, on_device(): lax.all_gather(w_out, ('dp', 'rep'), axis=0, tiled=True)  147 us
    all_to_all x1, waiting for transfers between devices, _reach_zones(): jax.lax.all_to_all(jnp.stack(jax.lax.axis_size(net_axis) * [vec], 0), net...  130 us
    psum x1, blocking collectives, on_device(): lax.psum(jnp.sum(centred * centred * row_weight, axis=0), ('dp', 'rep'))  74.3 us
    psum x1, blocking collectives, on_device(): lax.psum(jnp.sum(convolved * row_weight, axis=0), ('dp', 'rep'))  72.6 us
    reduce_sum x1, other arithmetic, on_device(): jnp.sum(convolved * row_weight, axis=0)  38.2 us
    all_to_all x1, starting transfers between devices, _reach_zones(): jax.lax.all_to_all(jnp.stack(jax.lax.axis_size(net_axis) * [vec], 0), net...  16.5 us
    reshape x1, local copies, waits for them, and re-layouts, _reach_zones(): long_array = jnp.concatenate(opened, 0)  14.2 us
    dot_general x1, matrix products, project_in(): return jnp.dot(normed, weight_rows, preferred_element_type=jnp.float32)  11.3 us
  transfers between devices with their start and end apart: 2, of which 2 were waited for; matrix products, arithmetic and copies ran while one was open for 2% of the time, Pallas kernels for 0%

profile of v1, /device:TPU:1, one launch (start us, length us, event | category | flops | bytes accessed | tf_op | source)
XLA Modules:
  0.0 553.9 jit_solution(557869866906929020)
XLA Ops:
  6.5 6.9 %stack.2 = bf16[256,6,3072]{2,1,0:T(8,128)(2,1)} broadcast(bf16[6,3072]{1,0:T(8,128)(2,1)} %param.13), dimensions={1,2} | broadcast | bytes 9474048 | tf_op jit(solution)/shard_map/stack | solution.py:11
  13.4 0.0 copy-start.7
  13.4 0.0 copy-start.2
  13.4 0.0 copy-start
  13.4 16.5 %all-to-all-start = ((bf16[256,6,3072]{2,1,0:T(8,128)(2,1)}), bf16[256,6,3072]{2,1,0:T(8,128)(2,1)}, u32[]{:S(2)}, u32[]{:S(2)}) async-start(bf16[256,6,3072]{2,1,0:T(8,128)(2,1)} %stack.2), calls=%async_computation | async-start | bytes 25165824 | tf_op jit(solution)/shard_map/all_to_all | solution.py:11
  29.9 0.0 all-gather.3.cloned.1.call-start
  30.0 0.7 all-gather.3.cloned.1.call-update
  30.7 0.0 copy-done.7
  30.7 0.6 reduce_sum.54
  31.3 0.2 reduce-window.8
  31.5 0.6 iota_compare_fusion.1
  32.2 0.7 fusion.27
  32.8 0.1 convert_reduce_fusion.1
  32.9 0.0 copy-done.2
  32.9 0.2 slice_reduce_fusion.29
  33.1 0.3 slice_reduce_fusion.30
  33.4 0.1 slice_compare_fusion.26
  33.5 0.0 copy-done
  33.5 0.4 convert_reduce_fusion
  34.0 0.9 fusion.3
  34.8 0.1 slice_compare_fusion.29
  34.9 0.1 slice_compare_fusion.28
  35.0 0.1 slice_compare_fusion.27
  35.1 147.1 %all-gather.3.cloned.1.call-done = bf16[256,6,1536]{2,1,0:T(8,128)(2,1)} async-done(((bf16[1,6,1536]{2,1,0:T(8,128)(2,1)}), bf16[256,6,1536]{2,1,0:T(8,128)(2,1)}) %all-gather.3.cloned.1.call-update) | async-done | bytes 4718608 | tf_op jit(solution)/shard_map/all_gather | solution.py:58
  182.2 8.4 %reshape.118 = bf16[1536,1536]{1,0:T(8,128)(2,1)} reshape(bf16[256,6,1536]{2,1,0:T(8,128)(2,1)} %all-gather.3.cloned.1.call-done) | data formatting | bytes 9437184
  190.6 0.0 copy-start.3
  190.6 0.0 copy-start.4
  190.6 130.3 %all-to-all-done = bf16[256,6,3072]{2,1,0:T(8,128)(2,1)} async-done(((bf16[256,6,3072]{2,1,0:T(8,128)(2,1)}), bf16[256,6,3072]{2,1,0:T(8,128)(2,1)}, u32[]{:S(2)}, u32[]{:S(2)}) %all-to-all-start) | async-done | bytes 9437216 | tf_op jit(solution)/shard_map/all_to_all | solution.py:11
  321.0 14.2 %reshape.116 = bf16[1536,3072]{1,0:T(8,128)(2,1)} reshape(bf16[256,6,3072]{2,1,0:T(8,128)(2,1)} %all-to-all-done) | data formatting | bytes 18874368 | tf_op jit(solution)/shard_map/reshape | solution.py:12
  335.2 0.0 copy-done.3
  335.2 0.0 copy-done.4
  335.2 11.3 %fusion.17 = f32[896,3072]{1,0:T(8,128)S(1)} fusion(bf16[1536,3072]{1,0:T(8,128)(2,1)} %reshape.116, bf16[1,896,1536]{2,1,0:T(8,128)(2,1)S(1)} %copy-done, f32[1536]{0:T(1024)S(1)} %copy-done.3, f32[1536]{0:T(1024)S(1)} %copy-done.4, f32[896]{0:T(1024)S(1)} %add_rsqrt_fusion.1, f32[896]{0:T(1024)S(1)} %broadcast_multiply_fusion.1), kind=kOutput, calls=%fused_computation.25 | convolution fusion | flops 8463974400 | bytes 23219200 | tf_op jit(solution)/shard_map/dot_general | solution.py:40
  346.5 1.5 fusion.13
  348.0 0.0 copy-start.5
  348.0 0.0 copy-start.6
  348.1 38.2 %multiply_reduce_fusion.1 = (f32[1536]{0:T(1024)S(1)}, f32[896,1536]{1,0:T(8,128)}) fusion(f32[896]{0:T(1024)S(1)} %fusion.27, f32[1536]{0:T(1024)S(1)} %get-tuple-element.34, pred[896]{0:T(1024)(128)(4,1)S(1)} %get-tuple-element.67, f32[1536]{0:T(1024)S(1)} %get-tuple-element.35, pred[896]{0:T(1024)(128)(4,1)S(1)} %get-tuple-element.39, ...), kind=kLoop, calls=%fused_computation.19 | loop fusion | flops 170654208 | bytes 8484608 | tf_op jit(solution)/shard_map/reduce_sum | solution.py:69
  386.3 0.0 copy-start.1
  386.3 72.6 %psum.14 = f32[1536]{0:T(1024)S(1)} all-reduce(f32[1536]{0:T(1024)S(1)} %get-tuple-element.36), channel_id=1, replica_groups=mesh['dp'=64,'rep'=4] {'dp','rep'}, use_global_device_ids=true, to_apply=%region_6.7 | all-reduce | flops 1536 | bytes 12288 | tf_op jit(solution)/shard_map/psum | solution.py:69
  458.9 3.3 multiply_reduce_fusion
  462.2 74.3 %psum.15 = f32[1536]{0:T(1024)S(1)} all-reduce(f32[1536]{0:T(1024)S(1)} %multiply_reduce_fusion), channel_id=1, replica_groups=mesh['dp'=64,'rep'=4] {'dp','rep'}, use_global_device_ids=true, to_apply=%region_8.9 | all-reduce | flops 1536 | bytes 12288 | tf_op jit(solution)/shard_map/psum | solution.py:71
  536.5 0.0 copy-done.5
  536.5 0.0 copy-done.6
  536.5 0.0 copy-done.1
  536.6 10.5 %fusion.15 = bf16[1,896,1536]{2,1,0:T(8,128)(2,1)} fusion(bf16[1536,1536]{1,0:T(8,128)(2,1)} %reshape.118, bf16[1,896,1536]{2,1,0:T(8,128)(2,1)S(1)} %copy-done.1, f32[896,1536]{1,0:T(8,128)} %get-tuple-element.37, f32[1536]{0:T(1024)S(1)} %copy-done.5, f32[1536]{0:T(1024)S(1)} %copy-done.6, f32[1536]{0:T(1024)S(1)} %add_rsqrt_fusion, ...), kind=kOutput, calls=%fused_computation.23 | convolution fusion | flops 4245749760 | bytes 15754112 | tf_op jit(solution)/shard_map/dot_general | solution.py:44
  (4 shorter events, 0.0 us)
Async XLA Ops:
  13.4 17.3 %copy-start.7 = (s32[1,1,4]{2,1,0:T(1,128)S(1)}, s32[1,1,4]{2,1,0:T(1,128)}, u32[]{:S(2)}) copy-start(s32[1,1,4]{2,1,0:T(1,128)} %param.10) | copy-start | bytes 52
  13.4 19.5 %copy-start.2 = (f32[31,1536]{1,0:T(8,128)S(1)}, f32[31,1536]{1,0:T(8,128)}, u32[]{:S(2)}) copy-start(f32[31,1536]{1,0:T(8,128)} %param.14) | copy-start | bytes 571396
  13.4 20.1 %copy-start = (bf16[1,896,1536]{2,1,0:T(8,128)(2,1)S(1)}, bf16[1,896,1536]{2,1,0:T(8,128)(2,1)}, u32[]{:S(2)}) copy-start(bf16[1,896,1536]{2,1,0:T(8,128)(2,1)} %param.9) | copy-start | bytes 8257540
  13.4 307.6 %all-to-all-start = ((bf16[256,6,3072]{2,1,0:T(8,128)(2,1)}), bf16[256,6,3072]{2,1,0:T(8,128)(2,1)}, u32[]{:S(2)}, u32[]{:S(2)}) async-start(bf16[256,6,3072]{2,1,0:T(8,128)(2,1)} %stack.2), calls=%async_computation | async-start | bytes 25165824 | tf_op jit(solution)/shard_map/all_to_all | solution.py:11
  29.9 152.3 %all-gather.3.cloned.1.call-start = ((), (), s32[]{:S(2)}) async-start(), calls=%async_computation.1 | async-start | bytes 6316032 | tf_op jit(solution)/shard_map/all_gather | solution.py:58
  190.6 144.5 %copy-start.3 = (f32[1536]{0:T(1024)S(1)}, f32[1536]{0:T(1024)}, u32[]{:S(2)}) copy-start(f32[1536]{0:T(1024)} %param.12) | copy-start | bytes 18436
  190.6 144.5 %copy-start.4 = (f32[1536]{0:T(1024)S(1)}, f32[1536]{0:T(1024)}, u32[]{:S(2)}) copy-start(f32[1536]{0:T(1024)} %param.11) | copy-start | bytes 18436
  348.0 188.5 %copy-start.5 = (f32[1536]{0:T(1024)S(1)}, f32[1536]{0:T(1024)}, u32[]{:S(2)}) copy-start(f32[1536]{0:T(1024)} %param.16) | copy-start | bytes 18436
  348.0 188.5 %copy-start.6 = (f32[1536]{0:T(1024)S(1)}, f32[1536]{0:T(1024)}, u32[]{:S(2)}) copy-start(f32[1536]{0:T(1024)} %param.15) | copy-start | bytes 18436
  386.3 150.3 %copy-start.1 = (bf16[1,896,1536]{2,1,0:T(8,128)(2,1)S(1)}, bf16[1,896,1536]{2,1,0:T(8,128)(2,1)}, u32[]{:S(2)}) copy-start(bf16[1,896,1536]{2,1,0:T(8,128)(2,1)} %param.9) | copy-start | bytes 8257540
Sparse Core Ops, SparseCore 0:
  34.6 147.5 all-gather.2
